TPU v7x, 512 devices: a whole 4x8x8 slice. The times are simulated.
512 devices in a mesh: aux: 8 (over z), ao: 16 (over y, core), orb: 4 (over x).
Axes of the slice: x: 4, y: 8, z: 8, core: 2. Of those that a mesh axis runs over, the one named last changes fastest.
Arguments:
- integrals: bfloat16 [128, 16, 4, 128, 128], P('aux', 'ao', None, 'orb'), may hold values from -6 to 6
- partner: int32 [16, 4], P('ao'), may hold values from 0 to 15
- pair_count: int32 [16], P('ao'), may hold values from 1 to 4
- occupied_coeff: bfloat16 [2048, 512], P('ao', 'orb'), may hold values from -0.25 to 0.25
- occupied_domain: int32 [16, 4], P('ao', 'orb'), may hold values 0 or 1
- virtual_coeff: bfloat16 [2048, 8192], P('aux', 'ao'), may hold values from -0.125 to 0.125
- virtual_domain: int32 [16, 64], P(None, 'ao'), may hold values 0 or 1
Outputs:
- transformed: bfloat16 [128, 512, 8192], P('aux', 'orb', 'ao')
All inputs are finite; a program needn't handle non-finite values. No bound on the sum of `occupied_domain` or of `virtual_domain` on one device may be relied on, other than what follows from the above.
Results may differ from a plain program's by a relative error of at most 0.0049.
Values may be sent and summed in bfloat16 or wider, within the bound.
A program may use at most 64 MiB of HBM per device.

v0:
```python
import jax
import jax.numpy as jnp
from jax import lax
from jax.sharding import PartitionSpec as P


def local(
    integrals, partner, pair_count, occupied_coeff, occupied_domain, virtual_coeff, virtual_domain
):
    block_size = integrals.shape[4]
    slab_rows = integrals.shape[0]
    slot_count = integrals.shape[2]
    occ_width = occupied_coeff.shape[1]
    occ_local = occupied_coeff * occupied_domain.astype(jnp.bfloat16)
    all_occ = lax.all_gather(occ_local, "ao", axis=0, tiled=True)
    all_ints = lax.all_gather(integrals, "orb", axis=3, tiled=True)
    vir_blocks = virtual_coeff.shape[0] // block_size
    first = lax.axis_index("aux") * vir_blocks
    dom = lax.dynamic_slice_in_dim(virtual_domain, first, vir_blocks, axis=0).astype(jnp.bfloat16)
    dom = jnp.repeat(jnp.repeat(dom, block_size, axis=0), block_size, axis=1)
    vir_masked = lax.all_gather(virtual_coeff * dom, "aux", axis=0, tiled=True)
    picked = all_occ.reshape(-1, block_size, occ_width)[partner[0]]
    slots = jnp.arange(slot_count, dtype=jnp.int32)
    live = (slots < pair_count[0]).astype(jnp.bfloat16)
    picked = picked * live[:, None, None]
    half = jnp.einsum(
        "kri,pkrv->piv", picked, all_ints[:, 0], preferred_element_type=jnp.float32
    ).astype(jnp.bfloat16)
    piece = lax.all_gather(half, "ao", axis=2, tiled=True)
    flat = piece.reshape(slab_rows * occ_width, piece.shape[2])
    product = jnp.dot(flat, vir_masked, preferred_element_type=jnp.float32)
    return product.reshape(slab_rows, occ_width, -1).astype(jnp.bfloat16)


def solution(mesh):
    placed = (
        P("aux", "ao", None, "orb", None),
        P("ao", None),
        P("ao"),
        P("ao", "orb"),
        P("ao", "orb"),
        P("aux", "ao"),
        P(None, "ao"),
    )
    return jax.shard_map(
        local, mesh=mesh, in_specs=placed, out_specs=P("aux", "orb", "ao"), check_vma=False
    )
```

profile of v0, /device:TPU:1, one launch (start us, length us, event | category | flops | bytes accessed | tf_op | source)
XLA Modules:
  0.0 183.8 jit_solution(8361173918025073191)
XLA Ops:
  6.5 0.0 all-gather.4.cloned.1.call-start
  6.5 0.7 all-gather.4.cloned.1.call-update
  7.3 0.0 all-gather.8.cloned.1.call-start
  7.3 0.8 dynamic-slice_convert_fusion
  8.1 0.1 copy.8
  8.2 0.3 broadcast_in_dim.9
  8.5 1.7 bitcast_multiply_fusion
  10.2 0.0 all-gather.8.cloned.1.call-update
  10.3 0.0 all-gather.6.cloned.1.call-start
  11.6 0.7 fusion.19
  12.3 0.8 broadcast_multiply_fusion
  13.0 22.4 %all_gather.12 = bf16[2048,128]{1,0:T(8,128)(2,1)S(1)} all-gather(bf16[128,128]{1,0:T(8,128)(2,1)S(1)} %broadcast_multiply_fusion), channel_id=1, replica_groups=mesh['aux'=8,'ao'=16,'orb'=4] {'ao'}, dimensions={0}, use_global_device_ids=true | all-gather | bytes 557056 | tf_op jit(solution)/shard_map/all_gather | solution.py:15
  35.4 0.6 gather_fusion
  36.0 14.8 %all-gather.4.cloned.1.call-done = bf16[16,1,4,128,128]{4,3,2,1,0:T(8,128)(2,1)} async-done(((bf16[16,1,4,32,128]{4,3,2,1,0:T(8,128)(2,1)}), bf16[16,1,4,128,128]{4,3,2,1,0:T(8,128)(2,1)}) %all-gather.4.cloned.1.call-update) | async-done | bytes 2097168 | tf_op jit(solution)/shard_map/all_gather | solution.py:16
  50.9 2.9 %fusion.13 = bf16[16,128,128]{2,1,0:T(8,128)(2,1)} fusion(bf16[16,1,4,128,128]{4,3,2,1,0:T(8,128)(2,1)} %all-gather.4.cloned.1.call-done, bf16[4,128,128]{2,1,0:T(8,128)(2,1)S(1)} %gather_fusion, bf16[4]{0:T(256)(128)(2,1)S(1)} %compare_convert_fusion), kind=kOutput, calls=%fused_computation.8 | convolution fusion | flops 268959744 | bytes 2752520 | tf_op jit(solution)/shard_map/kri,pkrv->piv/dot_general | solution.py:26
  53.8 0.0 all-gather.6.cloned.1.call-update
  53.8 39.3 %all-gather.8.cloned.1.call-done = bf16[2048,512]{1,0:T(8,128)(2,1)} async-done(((bf16[256,512]{1,0:T(8,128)(2,1)}), bf16[2048,512]{1,0:T(8,128)(2,1)}) %all-gather.8.cloned.1.call-update) | async-done | bytes 2097168 | tf_op jit(solution)/shard_map/all_gather | solution.py:21
  93.1 74.3 %all-gather.6.cloned.1.call-done = bf16[16,128,2048]{2,1,0:T(8,128)(2,1)} async-done(((bf16[16,128,128]{2,1,0:T(8,128)(2,1)}), bf16[16,128,2048]{2,1,0:T(8,128)(2,1)}) %all-gather.6.cloned.1.call-update) | async-done | bytes 8388624 | tf_op jit(solution)/shard_map/all_gather | solution.py:29
  167.4 9.8 %fusion.4 = bf16[16,128,512]{2,1,0:T(8,128)(2,1)} fusion(bf16[16,128,2048]{2,1,0:T(8,128)(2,1)} %all-gather.6.cloned.1.call-done, bf16[2048,512]{1,0:T(8,128)(2,1)} %all-gather.8.cloned.1.call-done), kind=kOutput, calls=%fused_computation.5 | convolution fusion | flops 4296015872 | bytes 12582912 | tf_op jit(solution)/shard_map/dot_general | solution.py:31
  (3 shorter events, 0.0 us)
Async XLA Ops:
  6.5 44.3 %all-gather.4.cloned.1.call-start = ((), (), s32[]{:S(2)}) async-start(), calls=%async_computation | async-start | bytes 2621440 | tf_op jit(solution)/shard_map/all_gather | solution.py:16
  7.3 85.9 %all-gather.8.cloned.1.call-start = ((), (), s32[]{:S(2)}) async-start(), calls=%async_computation.2 | async-start | bytes 2359296 | tf_op jit(solution)/shard_map/all_gather | solution.py:21
  10.3 157.2 %all-gather.6.cloned.1.call-start = ((), (), s32[]{:S(2)}) async-start(), calls=%async_computation.1 | async-start | bytes 8912896 | tf_op jit(solution)/shard_map/all_gather | solution.py:29
Sparse Core Ops, SparseCore 0:
  9.4 41.3 all-gather.3
  52.9 40.1 all-gather.7
  95.2 72.2 all-gather.5
where the time goes:
time: 184 us
  waiting for transfers between devices  129 us (70%)
  blocking collectives  22.4 us (12%)
  between operations  14.4 us (8%)
  matrix products  12.7 us (7%)
  other arithmetic  3.9 us (2%)
    all_gather x1, waiting for transfers between devices, local(): piece = lax.all_gather(half, 'ao', axis=2, tiled=True)  74.3 us
    all_gather x1, waiting for transfers between devices, local(): vir_masked = lax.all_gather(virtual_coeff * dom, 'aux', axis=0, tiled=True)  39.3 us
    all_gather x1, blocking collectives, local(): all_occ = lax.all_gather(occ_local, 'ao', axis=0, tiled=True)  22.4 us
    all_gather x1, waiting for transfers between devices, local(): all_ints = lax.all_gather(integrals, 'orb', axis=3, tiled=True)  14.8 us
    dot_general x1, matrix products, local(): product = jnp.dot(flat, vir_masked, preferred_element_type=jnp.float32)  9.82 us
  transfers between devices with their start and end apart: 3, of which 3 were waited for; matrix products, arithmetic and copies ran while one was open for 4% of the time, Pallas kernels for 0%

commit v1 on v0

--- a/solution.py
+++ b/solution.py
@@ -2,6 +2,13 @@
 import jax.numpy as jnp
 from jax import lax
 from jax.sharding import PartitionSpec as P
+
+
+def all_by_exchange(x, axis, along):
+    size = lax.axis_size(axis)
+    blocks = jnp.stack([x for _ in range(size)])
+    blocks = lax.all_to_all(blocks, axis, split_axis=0, concat_axis=0)
+    return jnp.concatenate(blocks, axis=along)
 
 
 def local(
@@ -18,7 +25,7 @@
     first = lax.axis_index("aux") * vir_blocks
     dom = lax.dynamic_slice_in_dim(virtual_domain, first, vir_blocks, axis=0).astype(jnp.bfloat16)
     dom = jnp.repeat(jnp.repeat(dom, block_size, axis=0), block_size, axis=1)
-    vir_masked = lax.all_gather(virtual_coeff * dom, "aux", axis=0, tiled=True)
+    vir_masked = all_by_exchange(virtual_coeff * dom, "aux", 0)
     picked = all_occ.reshape(-1, block_size, occ_width)[partner[0]]
     slots = jnp.arange(slot_count, dtype=jnp.int32)
     live = (slots < pair_count[0]).astype(jnp.bfloat16)

time: 184 us -> 139 us (0.76)
  waiting for transfers between devices: 129 us -> 30.7 us
  blocking collectives: 22.4 us -> 78.9 us
  other arithmetic: 3.9 us -> 1.56 us
    all_gather x1, waiting for transfers between devices: 74.3 us -> 12.1 us  [local(): piece = lax.all_gather(half, 'ao', axis=2, tiled=True)]
    all_to_all x0 -> x1, blocking collectives: none -> 56.5 us  [all_by_exchange(): blocks = lax.all_to_all(blocks, axis, split_axis=0, concat_axis=0)]
    all_gather x1 -> x0, waiting for transfers between devices: 39.3 us -> none  [local(): vir_masked = lax.all_gather(virtual_coeff * dom, 'aux', axis=0, tiled=True)]
    all_gather x1, waiting for transfers between devices: 14.8 us -> 17.9 us  [local(): all_ints = lax.all_gather(integrals, 'orb', axis=3, tiled=True)]
  transfers between devices with their start and end apart: 3 -> 2, of which waited for: 3 -> 2; matrix products, arithmetic and copies ran while one was open for 4% -> 2% of each run, Pallas kernels for 0% -> 0%
where the time goes in v1:
time: 139 us
  blocking collectives  78.9 us (57%)
  waiting for transfers between devices  30.7 us (22%)
  between operations  14.8 us (11%)
  matrix products  12 us (9%)
  other arithmetic  1.56 us (1%)
    all_to_all x1, blocking collectives, all_by_exchange(): blocks = lax.all_to_all(blocks, axis, split_axis=0, concat_axis=0)  56.5 us
    all_gather x1, blocking collectives, local(): all_occ = lax.all_gather(occ_local, 'ao', axis=0, tiled=True)  22.4 us
    all_gather x1, waiting for transfers between devices, local(): all_ints = lax.all_gather(integrals, 'orb', axis=3, tiled=True)  17.9 us
    all_gather x1, waiting for transfers between devices, local(): piece = lax.all_gather(half, 'ao', axis=2, tiled=True)  12.1 us
    dot_general x1, matrix products, local(): product = jnp.dot(flat, vir_masked, preferred_element_type=jnp.float32)  9.07 us
    dot_general x1, matrix products, local(): jnp.einsum('kri,pkrv->piv', picked, all_ints[:, 0], preferred_element_typ...  2.94 us
  transfers between devices with their start and end apart: 2, of which 2 were waited for; matrix products, arithmetic and copies ran while one was open for 2% of the time, Pallas kernels for 0%

profile of v1, /device:TPU:1, one launch (start us, length us, event | category | flops | bytes accessed | tf_op | source)
XLA Modules:
  0.0 139.2 jit_solution(8377472458960383007)
XLA Ops:
  6.5 0.0 all-gather.3.cloned.1.call-start
  6.5 0.7 all-gather.3.cloned.1.call-update
  7.3 0.0 all-gather.5.cloned.1.call-start
  8.6 0.7 fusion.14
  9.3 0.0 copy-start.1
  9.3 0.8 broadcast_multiply_fusion
  10.0 22.4 %all_gather.9 = bf16[2048,128]{1,0:T(8,128)(2,1)S(1)} all-gather(bf16[128,128]{1,0:T(8,128)(2,1)S(1)} %broadcast_multiply_fusion), channel_id=1, replica_groups=mesh['aux'=8,'ao'=16,'orb'=4] {'ao'}, dimensions={0}, use_global_device_ids=true | all-gather | bytes 557056 | tf_op jit(solution)/shard_map/all_gather | solution.py:22
  32.4 0.0 copy-start
  32.4 0.6 gather_fusion
  33.0 17.9 %all-gather.3.cloned.1.call-done = bf16[16,1,4,128,128]{4,3,2,1,0:T(8,128)(2,1)} async-done(((bf16[16,1,4,32,128]{4,3,2,1,0:T(8,128)(2,1)}), bf16[16,1,4,128,128]{4,3,2,1,0:T(8,128)(2,1)}) %all-gather.3.cloned.1.call-update) | async-done | bytes 2097168 | tf_op jit(solution)/shard_map/all_gather | solution.py:23
  50.9 2.9 %fusion.8 = bf16[16,128,128]{2,1,0:T(8,128)(2,1)} fusion(bf16[16,1,4,128,128]{4,3,2,1,0:T(8,128)(2,1)} %all-gather.3.cloned.1.call-done, bf16[4,128,128]{2,1,0:T(8,128)(2,1)S(1)} %gather_fusion, bf16[4]{0:T(256)(128)(2,1)S(1)} %compare_convert_fusion), kind=kOutput, calls=%fused_computation.6 | convolution fusion | flops 268959744 | bytes 2752520 | tf_op jit(solution)/shard_map/kri,pkrv->piv/dot_general | solution.py:33
  53.8 0.0 all-gather.5.cloned.1.call-update
  53.8 0.0 copy-done.1
  53.8 0.1 dynamic-slice_convert_fusion
  53.9 0.1 copy.8
  54.0 0.3 broadcast_in_dim.9
  54.4 0.0 copy-done
  54.4 0.2 stack.2
  54.6 56.5 %all_to_all.5 = bf16[8,256,512]{2,1,0:T(8,128)(2,1)S(1)} all-to-all(bf16[8,256,512]{2,1,0:T(8,128)(2,1)S(1)} %stack.2), channel_id=1, replica_groups=mesh['aux'=8,'ao'=16,'orb'=4] {'aux'}, dimensions={0} | all-to-all | bytes 4194304 | tf_op jit(solution)/shard_map/all_to_all | solution.py:10
  111.1 12.1 %all-gather.5.cloned.1.call-done = bf16[16,128,2048]{2,1,0:T(8,128)(2,1)} async-done(((bf16[16,128,128]{2,1,0:T(8,128)(2,1)}), bf16[16,128,2048]{2,1,0:T(8,128)(2,1)}) %all-gather.5.cloned.1.call-update) | async-done | bytes 8388624 | tf_op jit(solution)/shard_map/all_gather | solution.py:36
  123.2 9.1 %convolution_convert_fusion = bf16[16,128,512]{2,1,0:T(8,128)(2,1)} fusion(bf16[16,128,2048]{2,1,0:T(8,128)(2,1)} %all-gather.5.cloned.1.call-done, bf16[2048,512,1]{1,0,2:T(8,128)(2,1)S(1)} %bitcast.38), kind=kOutput, calls=%fused_computation.3 | convolution fusion | flops 4296015872 | bytes 12582912 | tf_op jit(solution)/shard_map/dot_general | solution.py:38
  (4 shorter events, 0.1 us)
Async XLA Ops:
  6.5 44.3 %all-gather.3.cloned.1.call-start = ((), (), s32[]{:S(2)}) async-start(), calls=%async_computation.1 | async-start | bytes 2621440 | tf_op jit(solution)/shard_map/all_gather | solution.py:23
  7.3 116.0 %all-gather.5.cloned.1.call-start = ((), (), s32[]{:S(2)}) async-start(), calls=%async_computation.2 | async-start | bytes 8912896 | tf_op jit(solution)/shard_map/all_gather | solution.py:36
  9.3 44.6 %copy-start.1 = (s32[16,4]{0,1:T(4,128)S(1)}, s32[16,4]{0,1:T(4,128)}, u32[]{:S(2)}) copy-start(s32[16,4]{0,1:T(4,128)} %param.13) | copy-start | bytes 772
  32.4 22.0 %copy-start = (bf16[256,512]{1,0:T(8,128)(2,1)S(1)}, bf16[256,512]{1,0:T(8,128)(2,1)}, u32[]{:S(2)}) copy-start(bf16[256,512]{1,0:T(8,128)(2,1)} %param.12) | copy-start | bytes 786436
Sparse Core Ops, SparseCore 0:
  9.4 41.3 all-gather.2
  53.9 69.2 all-gather.4
